TPU v7x, 256 devices: a whole 4x4x8 slice. The times are simulated.
256 devices in a mesh: sector: 32 (over x, z_lo, core), layer: 8 (over y, z_hi).
Axes of the slice: x: 4, y: 4, z: 8 (z_hi: 2, z_lo: 4; z = z_hi * 4 + z_lo), core: 2. Of those that a mesh axis runs over, the one named last changes fastest.
Arguments:
- rotor_state: float32 [5, 8, 128, 16384], P(None, None, 'layer', 'sector'), may hold values from -1.5 to 4, as said below
- cavity_state: float32 [5, 4, 128, 16384], P(None, None, 'layer', 'sector'), may hold values from -1.5 to 4, as said below
- block_map: int32 [32], replicated, may hold values from 0 to 31, each once
- rotor_offset: int32 [1], replicated, may hold values from 0 to 511
Outputs:
- rotor_next: float32 [5, 8, 128, 16384], P(None, None, 'layer', 'sector')
- cavity_next: float32 [5, 4, 128, 16384], P(None, None, 'layer', 'sector')
Inputs may be any that keep to these rules, and one draw needn't show every extreme that they name: `rotor_state`: component 0 lies in 0.5 to 1.5, components 1 to 3 in -1.5 to 1.5, component 4 in 2 to 4. `cavity_state`: component 0 lies in 0.5 to 1.5, components 1 to 3 in -1.5 to 1.5, component 4 in 2 to 4. `block_map`: each of 0 to 31 once.
All inputs are finite; a program needn't handle non-finite values.
Results may differ from a plain program's by a relative error of at most 0.00002.
Values sent between devices are 32-bit elements; how exact they have to be, the bound alone decides.
A program may use at most 192 MiB of HBM per device.

v0:
```python
import jax
import jax.numpy as jnp
from jax import lax
from jax.sharding import PartitionSpec as P

DIFFUSION = 0.05
COURANT = 0.1


def with_halo(cells, sides, width, closed):
    for axis, dim in sides:
        count = lax.axis_size(axis)
        ends = count if closed else count - 1
        head = lax.slice_in_dim(cells, 0, width, axis=dim)
        tail = lax.slice_in_dim(cells, cells.shape[dim] - width, cells.shape[dim], axis=dim)
        cells = jnp.concatenate(
            [
                lax.ppermute(tail, axis, [(i, (i + 1) % count) for i in range(ends)]),
                cells,
                lax.ppermute(head, axis, [((i + 1) % count, i) for i in range(ends)]),
            ],
            axis=dim,
        )
    return cells


def shifted(value, axis, steps):
    count = lax.axis_size(axis)
    pairs = [(source, (source + steps) % count) for source in range(count)]
    return lax.ppermute(value, axis, pairs)


def viscosity(density, energy):
    return 0.5 * (energy / density) ** 0.7


def region_update(region, seam_ghost, seam_last):
    cycle_padded = with_halo(region, (("sector", 3),), 1, True)
    radial_padded = with_halo(region, (("layer", 2),), 1, False)
    layer_here = lax.axis_index("layer")
    layers = lax.axis_size("layer")
    radial_rows = region.shape[2]
    viscous = viscosity(region[0], region[4])
    ghost_viscous = viscosity(seam_ghost[0], seam_ghost[4])
    if seam_last:
        extended = jnp.concatenate([region, seam_ghost[:, None]], axis=1)
        extended_mu = jnp.concatenate([viscous, ghost_viscous[None]], axis=0)
    else:
        extended = jnp.concatenate([seam_ghost[:, None], region], axis=1)
        extended_mu = jnp.concatenate([ghost_viscous[None], viscous], axis=0)
    face_axial = (
        0.5
        * (extended_mu[None, 1:] + extended_mu[None, :-1])
        * (extended[:, 1:] - extended[:, :-1])
    )
    empty_plane = jnp.zeros_like(face_axial[:, :1])
    if seam_last:
        axial_sum = face_axial - jnp.concatenate([empty_plane, face_axial[:, :-1]], axis=1)
    else:
        axial_sum = jnp.concatenate([face_axial[:, 1:], empty_plane], axis=1) - face_axial
    radial_mu = viscosity(radial_padded[0], radial_padded[4])
    face_radial = (
        0.5
        * (radial_mu[None, :, 1:] + radial_mu[None, :, :-1])
        * (radial_padded[:, :, 1:] - radial_padded[:, :, :-1])
    )
    face_index = jnp.arange(radial_rows + 1, dtype=jnp.int32)
    closed = (face_index == 0) & (layer_here == 0) | (face_index == radial_rows) & (
        layer_here == layers - 1
    )
    face_radial = jnp.where(closed[None, None, :, None], 0.0, face_radial)
    radial = face_radial[:, :, 1:] - face_radial[:, :, :-1]
    cycle_mu = viscosity(cycle_padded[0], cycle_padded[4])
    face_cycle = (
        0.5
        * (cycle_mu[None, ..., 1:] + cycle_mu[None, ..., :-1])
        * (cycle_padded[..., 1:] - cycle_padded[..., :-1])
    )
    cycle_sum = face_cycle[..., 1:] - face_cycle[..., :-1]
    velocity = cycle_padded[3] / cycle_padded[0]
    carried = velocity[None] * cycle_padded
    advected = -COURANT * 0.5 * (carried[..., 2:] - carried[..., :-2])
    return region + DIFFUSION * (axial_sum + radial + cycle_sum) + advected


def shards(rotor_state, cavity_state, block_map, rotor_offset):
    sectors = lax.axis_size("sector")
    position = lax.axis_index("sector")
    components = rotor_state.shape[0]
    radial_rows = rotor_state.shape[2]
    cycle_cells = rotor_state.shape[3]
    block_cells = cycle_cells // sectors
    offset_cells = rotor_offset[0]
    slot_index = jnp.arange(sectors, dtype=jnp.int32)
    rotor_seam = rotor_state[:, -1].reshape(components, radial_rows, sectors, block_cells)
    cavity_seam = cavity_state[:, 0]
    following = shifted(cavity_seam, "sector", -1)
    lifted = lax.dynamic_slice_in_dim(
        jnp.concatenate([cavity_seam, following], axis=2), offset_cells, cycle_cells, axis=2
    )
    lifted = lifted.reshape(components, radial_rows, sectors, block_cells)
    every_rotor = lax.all_gather(rotor_seam, "sector", axis=2, tiled=True)
    landed = jnp.take(every_rotor, (position - block_map) % sectors * sectors + slot_index, axis=2)
    every_cavity = lax.all_gather(lifted, "sector", axis=2, tiled=True)
    returned = jnp.take(
        every_cavity, (position + block_map) % sectors * sectors + slot_index, axis=2
    )
    landed_flat = landed.reshape(components, radial_rows, cycle_cells)
    preceding = shifted(landed_flat, "sector", 1)
    cavity_ghost = lax.dynamic_slice_in_dim(
        jnp.concatenate([preceding, landed_flat], axis=2),
        cycle_cells - offset_cells,
        cycle_cells,
        axis=2,
    )
    rotor_ghost = returned.reshape(components, radial_rows, cycle_cells)
    rotor_next = region_update(rotor_state, rotor_ghost, True)
    cavity_next = region_update(cavity_state, cavity_ghost, False)
    return (rotor_next, cavity_next)


def solution(mesh):
    placed = (P(None, None, "layer", "sector"), P(None, None, "layer", "sector"), P(), P())
    return jax.shard_map(
        shards,
        mesh=mesh,
        in_specs=placed,
        out_specs=(P(None, None, "layer", "sector"), P(None, None, "layer", "sector")),
        check_vma=False,
    )
```

profile of v0, /device:TPU:1, one launch (start us, length us, event | category | flops | bytes accessed | tf_op | source)
XLA Modules:
  0.0 520.8 jit_solution(2654275196244347219)
XLA Ops:
  8.6 1.8 copy.22
  10.5 1.0 copy-done.1
  11.5 3.3 collective-permute-start
  15.4 2.2 collective-permute-done
  18.2 1.8 copy.12
  20.3 5.6 %collective-permute-start.9 = (f32[5,4,16,1]{3,2,1,0:T(8,128)S(1)}, f32[5,4,16,1]{3,2,1,0:T(8,128)S(1)}, u32[]{:S(2)}, u32[]{:S(2)}) collective-permute-start(f32[5,4,16,1]{3,2,1,0:T(8,128)S(1)} %get-tuple-element.18), channel_id=1, source_target_pairs={{8,0},{16,8},{24,16},{32,24},{40,32},{48,40},{56,48},{64,56},{72,6... | collective-permute-start | bytes 3848 | tf_op jit(solution)/shard_map/ppermute | solution.py:20
  26.6 5.1 collective-permute-start.6
  31.8 1.3 collective-permute-start.7
  37.2 6.1 %collective-permute-start.4 = (f32[5,8,16,1]{3,2,1,0:T(8,128)}, f32[5,8,16,1]{3,2,1,0:T(8,128)S(1)}, u32[]{:S(2)}, u32[]{:S(2)}) collective-permute-start(f32[5,8,16,1]{3,2,1,0:T(8,128)} %get-tuple-element.12), channel_id=1, source_target_pairs={{8,0},{16,8},{24,16},{32,24},{40,32},{48,40},{56,48},{64,56},{72,6... | collective-permute-start | bytes 7688 | tf_op jit(solution)/shard_map/ppermute | solution.py:20
  43.3 8.2 %collective-permute-start.1 = (f32[5,8,1,512]{3,1,2,0:T(8,128)}, f32[5,8,1,512]{3,1,2,0:T(8,128)S(1)}, u32[]{:S(2)}, u32[]{:S(2)}) collective-permute-start(f32[5,8,1,512]{3,1,2,0:T(8,128)} %copy.24), channel_id=1, source_target_pairs={{0,1},{1,2},{2,3},{3,4},{4,5},{5,6},{6,7},{8,9},{9,10},{10,11},{11... | collective-permute-start | bytes 245768 | tf_op jit(solution)/shard_map/ppermute | solution.py:18
  52.3 1.3 broadcast_multiply_fusion.1
  53.6 1.5 collective-permute-start.2
  56.3 1.7 fusion.2
  58.0 1.8 broadcast_multiply_fusion
  60.0 1.2 fusion.12
  61.3 4.0 collective-permute-done.2
  65.8 1.8 fusion.1
  67.6 187.4 %all-gather.5.cloned.1.call-done = f32[5,16,1024,16]{3,1,2,0:T(8,128)} async-done(((f32[5,16,32,16]{3,1,2,0:T(8,128)}), f32[5,16,1024,16]{3,1,2,0:T(8,128)}) %all-gather.5.cloned.1.call-update) | async-done | bytes 5242896 | tf_op jit(solution)/shard_map/all_gather | solution.py:102
  255.0 3.0 gather_fusion.1
  258.0 230.7 %all-gather.3.cloned.1.call-done = f32[5,16,1024,16]{3,1,2,0:T(8,128)} async-done(((f32[5,16,32,16]{3,1,2,0:T(8,128)}), f32[5,16,1024,16]{3,1,2,0:T(8,128)}) %all-gather.3.cloned.1.call-update) | async-done | bytes 5242896 | tf_op jit(solution)/shard_map/all_gather | solution.py:104
  488.7 3.0 gather_fusion
  491.8 1.9 select_bitcast_fusion
  493.7 1.5 copy.14
  495.4 1.5 copy.23
  496.8 2.8 reshape.106
  499.7 1.4 collective-permute-start.5
  501.1 2.1 broadcast_in_dim_reshape.3
  504.0 1.1 mul.216
  505.6 1.0 copy-done.3
  507.7 2.1 fusion.4
  509.9 1.1 fusion.41
  512.5 1.4 fusion.15
  (73 shorter events, 14.0 us)
Async XLA Ops:
  7.2 247.8 %all-gather.5.cloned.1.call-start = ((), (), s32[]{:S(2)}) async-start(), calls=%async_computation.1 | async-start | bytes 43253760 | tf_op jit(solution)/shard_map/all_gather | solution.py:102
  10.4 1.1 copy-start.1
  10.4 478.3 %all-gather.3.cloned.1.call-start = ((), (), s32[]{:S(2)}) async-start(), calls=%async_computation | async-start | bytes 43253760 | tf_op jit(solution)/shard_map/all_gather | solution.py:104
  11.5 6.1 %collective-permute-start = (f32[5,16,512]{2,1,0:T(8,128)S(1)}, f32[5,16,512]{2,1,0:T(8,128)S(1)}, u32[]{:S(2)}, u32[]{:S(2)}) collective-permute-start(f32[5,16,512]{2,1,0:T(8,128)S(1)} %slice_bitcast_fusion), channel_id=1, source_target_pairs={{0,248},{8,0},{16,8},{24,16},{32,24},{40,32},{48,40},{56,48},{64,5... | collective-permute-start | bytes 491528 | tf_op jit(solution)/shard_map/ppermute | solution.py:30
  20.1 13.0 %copy-start = (f32[5,8,16,512]{3,2,1,0:T(8,128)S(1)}, f32[5,8,16,512]{3,2,1,0:T(8,128)}, u32[]{:S(2)}) copy-start(f32[5,8,16,512]{3,2,1,0:T(8,128)} %param.6) | copy-start | bytes 3932164
  20.1 13.9 %copy-start.10 = (s32[32]{0:T(128)S(1)}, s32[32]{0:T(128)}, u32[]{:S(2)}) copy-start(s32[32]{0:T(128)} %param.8) | copy-start | bytes 388
  20.2 17.0 %collective-permute-start.8 = (f32[5,4,16,1]{3,2,1,0:T(8,128)S(1)}, f32[5,4,16,1]{3,2,1,0:T(8,128)S(1)}, u32[]{:S(2)}, u32[]{:S(2)}) collective-permute-start(f32[5,4,16,1]{3,2,1,0:T(8,128)S(1)} %get-tuple-element.17), channel_id=1, source_target_pairs={{0,8},{8,16},{16,24},{24,32},{32,40},{40,48},{48,56},{56,64},{64,7... | collective-permute-start | bytes 3848 | tf_op jit(solution)/shard_map/ppermute | solution.py:18
  20.3 23.0 %collective-permute-start.9 = (f32[5,4,16,1]{3,2,1,0:T(8,128)S(1)}, f32[5,4,16,1]{3,2,1,0:T(8,128)S(1)}, u32[]{:S(2)}, u32[]{:S(2)}) collective-permute-start(f32[5,4,16,1]{3,2,1,0:T(8,128)S(1)} %get-tuple-element.18), channel_id=1, source_target_pairs={{8,0},{16,8},{24,16},{32,24},{40,32},{48,40},{56,48},{64,56},{72,6... | collective-permute-start | bytes 3848 | tf_op jit(solution)/shard_map/ppermute | solution.py:20
  26.6 33.2 %collective-permute-start.6 = (f32[5,4,1,512]{3,2,1,0:T(1,128)}, f32[5,4,1,512]{3,2,1,0:T(1,128)S(1)}, u32[]{:S(2)}, u32[]{:S(2)}) collective-permute-start(f32[5,4,1,512]{3,2,1,0:T(1,128)} %get-tuple-element.15), channel_id=1, source_target_pairs={{0,1},{1,2},{2,3},{3,4},{4,5},{5,6},{6,7},{8,9},{9,10},{10,11},{11... | collective-permute-start | bytes 122888 | tf_op jit(solution)/shard_map/ppermute | solution.py:18
  31.8 28.1 %collective-permute-start.7 = (f32[5,4,1,512]{3,2,1,0:T(1,128)}, f32[5,4,1,512]{3,2,1,0:T(1,128)S(1)}, u32[]{:S(2)}, u32[]{:S(2)}) collective-permute-start(f32[5,4,1,512]{3,2,1,0:T(1,128)} %get-tuple-element.16), channel_id=1, source_target_pairs={{1,0},{2,1},{3,2},{4,3},{5,4},{6,5},{7,6},{9,8},{10,9},{11,10},{12... | collective-permute-start | bytes 122888 | tf_op jit(solution)/shard_map/ppermute | solution.py:20
  34.0 19.6 %collective-permute-start.3 = (f32[5,8,16,1]{3,2,1,0:T(8,128)}, f32[5,8,16,1]{3,2,1,0:T(8,128)S(1)}, u32[]{:S(2)}, u32[]{:S(2)}) collective-permute-start(f32[5,8,16,1]{3,2,1,0:T(8,128)} %get-tuple-element.11), channel_id=1, source_target_pairs={{0,8},{8,16},{16,24},{24,32},{32,40},{40,48},{48,56},{56,64},{64,7... | collective-permute-start | bytes 7688 | tf_op jit(solution)/shard_map/ppermute | solution.py:18
  37.2 18.2 %collective-permute-start.4 = (f32[5,8,16,1]{3,2,1,0:T(8,128)}, f32[5,8,16,1]{3,2,1,0:T(8,128)S(1)}, u32[]{:S(2)}, u32[]{:S(2)}) collective-permute-start(f32[5,8,16,1]{3,2,1,0:T(8,128)} %get-tuple-element.12), channel_id=1, source_target_pairs={{8,0},{16,8},{24,16},{32,24},{40,32},{48,40},{56,48},{64,56},{72,6... | collective-permute-start | bytes 7688 | tf_op jit(solution)/shard_map/ppermute | solution.py:20
  43.3 18.0 %collective-permute-start.1 = (f32[5,8,1,512]{3,1,2,0:T(8,128)}, f32[5,8,1,512]{3,1,2,0:T(8,128)S(1)}, u32[]{:S(2)}, u32[]{:S(2)}) collective-permute-start(f32[5,8,1,512]{3,1,2,0:T(8,128)} %copy.24), channel_id=1, source_target_pairs={{0,1},{1,2},{2,3},{3,4},{4,5},{5,6},{6,7},{8,9},{9,10},{10,11},{11... | collective-permute-start | bytes 245768 | tf_op jit(solution)/shard_map/ppermute | solution.py:18
  52.3 1.3 copy-start.9
  53.6 11.7 %collective-permute-start.2 = (f32[5,8,1,512]{3,1,2,0:T(8,128)S(1)}, f32[5,8,1,512]{3,1,2,0:T(8,128)S(1)}, u32[]{:S(2)}, u32[]{:S(2)}) collective-permute-start(f32[5,8,1,512]{3,1,2,0:T(8,128)S(1)} %copy-done.9), channel_id=1, source_target_pairs={{1,0},{2,1},{3,2},{4,3},{5,4},{6,5},{7,6},{9,8},{10,9},{11,10},{12... | collective-permute-start | bytes 245768 | tf_op jit(solution)/shard_map/ppermute | solution.py:20
  499.7 5.4 %copy-start.7 = (f32[8,16,512]{2,1,0:T(8,128)S(1)}, f32[8,16,512]{2,1,0:T(8,128)}, u32[]{:S(2)}) copy-start(f32[8,16,512]{2,1,0:T(8,128)} %multiply_bitcast_fusion) | copy-start | bytes 786436
  499.7 10.2 %collective-permute-start.5 = (f32[5,16,512]{2,1,0:T(8,128)}, f32[5,16,512]{2,1,0:T(8,128)}, u32[]{:S(2)}, u32[]{:S(2)}) collective-permute-start(f32[5,16,512]{2,1,0:T(8,128)} %reshape.106), channel_id=1, source_target_pairs={{0,8},{8,16},{16,24},{24,32},{32,40},{40,48},{48,56},{56,64},{64,7... | collective-permute-start | bytes 491528 | tf_op jit(solution)/shard_map/ppermute | solution.py:30
  505.1 1.4 copy-start.3
  505.1 2.0 copy-start.4
  505.4 2.3 copy-start.2
  507.7 3.3 copy-start.8
  511.0 1.1 copy-start.5
  511.0 1.4 copy-start.6
Sparse Core Ops, SparseCore 0:
  10.6 244.3 all-gather.4
  256.9 231.8 all-gather.2
where the time goes:
time: 521 us
  waiting for transfers between devices  425 us (82%)
  starting transfers between devices  32.6 us (6%)
  local copies, waits for them, and re-layouts  29.2 us (6%)
  other arithmetic  19.2 us (4%)
  between operations  15 us (3%)
    all_gather x1, waiting for transfers between devices, shards(): every_cavity = lax.all_gather(lifted, 'sector', axis=2, tiled=True)  231 us
    all_gather x1, waiting for transfers between devices, shards(): every_rotor = lax.all_gather(rotor_seam, 'sector', axis=2, tiled=True)  187 us
    ppermute x4, starting transfers between devices, with_halo(): lax.ppermute(head, axis, [((i + 1) % count, i) for i in range(ends)])  14.5 us
    ppermute x4, starting transfers between devices, with_halo(): lax.ppermute(tail, axis, [(i, (i + 1) % count) for i in range(ends)])  13.4 us
  transfers between devices with their start and end apart: 12, of which 5 were waited for; matrix products, arithmetic and copies ran while one was open for 5% of the time, Pallas kernels for 0%

commit v1 on v0

--- a/solution.py
+++ b/solution.py
@@ -84,6 +84,15 @@
 
 
 def shards(rotor_state, cavity_state, block_map, rotor_offset):
+
+    def launch_results(state):
+        return jnp.concatenate(
+            jax.lax.all_to_all(
+                jnp.stack(jax.lax.psum(1, "sector") * [state], axis=0), "sector", 0, 0
+            ),
+            axis=2,
+        )
+
     sectors = lax.axis_size("sector")
     position = lax.axis_index("sector")
     components = rotor_state.shape[0]
@@ -101,7 +110,7 @@
     lifted = lifted.reshape(components, radial_rows, sectors, block_cells)
     every_rotor = lax.all_gather(rotor_seam, "sector", axis=2, tiled=True)
     landed = jnp.take(every_rotor, (position - block_map) % sectors * sectors + slot_index, axis=2)
-    every_cavity = lax.all_gather(lifted, "sector", axis=2, tiled=True)
+    every_cavity = launch_results(lifted)
     returned = jnp.take(
         every_cavity, (position + block_map) % sectors * sectors + slot_index, axis=2
     )

time: 521 us -> 498 us (0.956)
  waiting for transfers between devices: 425 us -> 275 us
  local copies, waits for them, and re-layouts: 29.2 us -> 124 us
  other arithmetic: 19.2 us -> 35.9 us
  starting transfers between devices: 32.6 us -> 43.9 us
    all_gather x1 -> x0, waiting for transfers between devices: 231 us -> none  [shards(): every_cavity = lax.all_gather(lifted, 'sector', axis=2, tiled=True)]
    ppermute x4, waiting for transfers between devices: 0.01 us -> 151 us  [with_halo(): lax.ppermute(tail, axis, [(i, (i + 1) % count) for i in range(ends)])]
    all_gather x1, waiting for transfers between devices: 187 us -> 112 us  [shards(): every_rotor = lax.all_gather(rotor_seam, 'sector', axis=2, tiled=True)]
    unnamed x24 -> x27, local copies, waits for them, and re-layouts: 5.74 us -> 54.4 us
    reshape x2, local copies, waits for them, and re-layouts: 2.27 us -> 46 us  [launch_results(): jnp.concatenate(jax.lax.all_to_all(jnp.stack(jax.lax.psum(1, 'sector') *...]
    all_to_all x0 -> x1, other arithmetic: none -> 16.7 us  [launch_results(): jax.lax.all_to_all(jnp.stack(jax.lax.psum(1, 'sector') * [state], axis=0)...]
    ppermute x4, starting transfers between devices: 14.5 us -> 2.76 us  [with_halo(): lax.ppermute(head, axis, [((i + 1) % count, i) for i in range(ends)])]
    all_to_all x0 -> x1, starting transfers between devices: none -> 11.2 us  [launch_results(): jax.lax.all_to_all(jnp.stack(jax.lax.psum(1, 'sector') * [state], axis=0)...]
  transfers between devices with their start and end apart: 12 -> 12, of which waited for: 5 -> 3; matrix products, arithmetic and copies ran while one was open for 5% -> 12% of each run, Pallas kernels for 0% -> 0%
where the time goes in v1:
time: 498 us; the launch traced here: 494 us
  waiting for transfers between devices  275 us (55%)
  local copies, waits for them, and re-layouts  124 us (25%)
  starting transfers between devices  43.9 us (9%)
  other arithmetic  35.9 us (7%)
  between operations  15.1 us (3%)
    ppermute x4, waiting for transfers between devices, with_halo(): lax.ppermute(tail, axis, [(i, (i + 1) % count) for i in range(ends)])  151 us
    all_gather x1, waiting for transfers between devices, shards(): every_rotor = lax.all_gather(rotor_seam, 'sector', axis=2, tiled=True)  112 us
    unnamed x27, local copies, waits for them, and re-layouts  54.4 us
    reshape x2, local copies, waits for them, and re-layouts, launch_results(): jnp.concatenate(jax.lax.all_to_all(jnp.stack(jax.lax.psum(1, 'sector') *...  46 us
    ppermute x4, starting transfers between devices, with_halo(): lax.ppermute(tail, axis, [(i, (i + 1) % count) for i in range(ends)])  17.1 us
    all_to_all x1, other arithmetic, launch_results(): jax.lax.all_to_all(jnp.stack(jax.lax.psum(1, 'sector') * [state], axis=0)...  16.7 us
    ppermute x2, starting transfers between devices, shifted(): return lax.ppermute(value, axis, pairs)  12.8 us
    ppermute x4, waiting for transfers between devices, with_halo(): lax.ppermute(head, axis, [((i + 1) % count, i) for i in range(ends)])  12.5 us
  transfers between devices with their start and end apart: 12, of which 3 were waited for; matrix products, arithmetic and copies ran while one was open for 12% of the time, Pallas kernels for 0%

profile of v1, /device:TPU:1, one launch (start us, length us, event | category | flops | bytes accessed | tf_op | source)
XLA Modules:
  0.0 493.8 jit_solution(11897845572943086959)
XLA Ops:
  8.1 3.3 collective-permute-start
  12.8 1.8 copy.25
  16.3 9.6 %broadcast_bitcast_fusion = f32[32,5,16,16,32]{4,3,2,1,0:T(8,128)} fusion(f32[5,16,32,16]{2,3,1,0:T(8,128)S(1)} %copy.13), kind=kLoop, calls=%fused_computation.119 | loop fusion | bytes 5406720
  25.9 18.7 %reshape.135 = f32[32,1,40960]{2,1,0:T(1,128)} reshape(f32[32,5,16,16,32]{4,3,2,1,0:T(8,128)} %broadcast_bitcast_fusion) | data formatting | bytes 10485760
  44.7 11.2 %all-to-all-start = ((f32[32,1,40960]{2,1,0:T(1,128)}), f32[32,1,40960]{2,1,0:T(1,128)}, u32[]{:S(2)}, u32[]{:S(2)}) async-start(f32[32,1,40960]{2,1,0:T(1,128)} %reshape.135), calls=%async_computation | async-start | bytes 10485760 | tf_op jit(solution)/shard_map/all_to_all | solution.py:90
  56.0 1.7 collective-permute-start.8
  58.4 6.2 %collective-permute-start.6 = (f32[5,4,1,512]{3,2,1,0:T(1,128)}, f32[5,4,1,512]{3,2,1,0:T(1,128)S(1)}, u32[]{:S(2)}, u32[]{:S(2)}) collective-permute-start(f32[5,4,1,512]{3,2,1,0:T(1,128)} %get-tuple-element.15), channel_id=1, source_target_pairs={{0,1},{1,2},{2,3},{3,4},{4,5},{5,6},{6,7},{8,9},{9,10},{10,11},{11... | collective-permute-start | bytes 122888 | tf_op jit(solution)/shard_map/ppermute | solution.py:18
  64.6 1.3 collective-permute-start.7
  66.9 2.0 collective-permute-start.3
  72.0 150.7 %collective-permute-done.8 = f32[5,4,16,1]{3,2,1,0:T(8,128)S(1)} collective-permute-done((f32[5,4,16,1]{3,2,1,0:T(8,128)S(1)}, f32[5,4,16,1]{3,2,1,0:T(8,128)S(1)}, u32[]{:S(2)}, u32[]{:S(2)}) %collective-permute-start.8) | collective-permute-done | bytes 1312 | tf_op jit(solution)/shard_map/ppermute | solution.py:18
  222.8 7.2 %collective-permute-start.1 = (f32[5,8,1,512]{3,1,2,0:T(8,128)}, f32[5,8,1,512]{3,1,2,0:T(8,128)S(1)}, u32[]{:S(2)}, u32[]{:S(2)}) collective-permute-start(f32[5,8,1,512]{3,1,2,0:T(8,128)} %copy.29), channel_id=1, source_target_pairs={{0,1},{1,2},{2,3},{3,4},{4,5},{5,6},{6,7},{8,9},{9,10},{10,11},{11... | collective-permute-start | bytes 245768 | tf_op jit(solution)/shard_map/ppermute | solution.py:18
  230.8 1.3 broadcast_multiply_fusion.1
  232.1 1.5 collective-permute-start.2
  233.6 12.4 %collective-permute-done.4 = f32[5,8,16,1]{3,2,1,0:T(8,128)S(1)} collective-permute-done((f32[5,8,16,1]{3,2,1,0:T(8,128)}, f32[5,8,16,1]{3,2,1,0:T(8,128)S(1)}, u32[]{:S(2)}, u32[]{:S(2)}) %collective-permute-start.4) | collective-permute-done | bytes 2592 | tf_op jit(solution)/shard_map/ppermute | solution.py:20
  247.0 1.7 fusion.2
  248.7 1.8 broadcast_multiply_fusion
  252.6 1.8 fusion.1
  254.3 111.9 %all-gather.2.cloned.1.call-done = f32[5,16,1024,16]{3,1,2,0:T(8,128)} async-done(((f32[5,16,32,16]{3,1,2,0:T(8,128)}), f32[5,16,1024,16]{3,1,2,0:T(8,128)}) %all-gather.2.cloned.1.call-update) | async-done | bytes 5242896 | tf_op jit(solution)/shard_map/all_gather | solution.py:111
  366.2 3.0 gather_fusion.1
  369.8 16.7 %reduce = f32[32,40960]{1,0:T(8,128)} reduce(f32[32,1,40960]{2,1,0:T(1,128)} %all-to-all-done, f32[]{:T(128)} %broadcast.148), dimensions={1}, to_apply=%all_to_all.3.reduce_sub_computation | reduce | bytes 10485764 | tf_op jit(solution)/shard_map/all_to_all | solution.py:90
  386.5 21.3 %reshape.136 = f32[32,5,16,16,32]{4,3,2,1,0:T(8,128)} reshape(f32[32,40960]{1,0:T(8,128)} %reduce) | data formatting | bytes 10485760
  407.7 16.1 %bitcast_bitcast_fusion = f32[5,16,32,32,16]{3,4,1,0,2:T(8,128)} fusion(f32[32,5,16,16,32]{4,3,2,1,0:T(8,128)} %reshape.136), kind=kLoop, calls=%fused_computation.118 | loop fusion | bytes 10485760 | tf_op jit(solution)/shard_map/reshape | solution.py:89
  423.8 30.0 %copy.27 = f32[5,16,32,32,16]{4,1,3,2,0:T(8,128)} copy(f32[5,16,32,32,16]{3,4,1,0,2:T(8,128)} %bitcast_bitcast_fusion) | data formatting | bytes 10485760 | tf_op jit(solution)/shard_map/reshape | solution.py:89
  453.8 3.0 gather_fusion
  456.8 1.9 select_bitcast_fusion
  458.8 1.5 copy.17
  460.4 1.5 copy.26
  461.9 2.8 reshape.112
  464.7 9.5 %collective-permute-start.5 = (f32[5,16,512]{2,1,0:T(8,128)}, f32[5,16,512]{2,1,0:T(8,128)}, u32[]{:S(2)}, u32[]{:S(2)}) collective-permute-start(f32[5,16,512]{2,1,0:T(8,128)} %reshape.112), channel_id=1, source_target_pairs={{0,8},{8,16},{16,24},{24,32},{32,40},{40,48},{48,56},{56,64},{64,7... | collective-permute-start | bytes 491528 | tf_op jit(solution)/shard_map/ppermute | solution.py:30
  474.2 2.1 broadcast_in_dim_reshape.3
  480.8 2.1 fusion.4
  485.6 1.4 fusion.15
  (79 shorter events, 19.7 us)
Async XLA Ops:
  7.2 359.1 %all-gather.2.cloned.1.call-start = ((), (), s32[]{:S(2)}) async-start(), calls=%async_computation.1 | async-start | bytes 43253760 | tf_op jit(solution)/shard_map/all_gather | solution.py:111
  8.1 7.2 %collective-permute-start = (f32[5,16,512]{2,1,0:T(8,128)S(1)}, f32[5,16,512]{2,1,0:T(8,128)S(1)}, u32[]{:S(2)}, u32[]{:S(2)}) collective-permute-start(f32[5,16,512]{2,1,0:T(8,128)S(1)} %slice_bitcast_fusion), channel_id=1, source_target_pairs={{0,248},{8,0},{16,8},{24,16},{32,24},{40,32},{48,40},{56,48},{64,5... | collective-permute-start | bytes 491528 | tf_op jit(solution)/shard_map/ppermute | solution.py:30
  44.7 11.2 %copy-start.1 = (f32[5,4,16,512]{3,2,1,0:T(8,128)S(1)}, f32[5,4,16,512]{3,2,1,0:T(8,128)}, u32[]{:S(2)}) copy-start(f32[5,4,16,512]{3,2,1,0:T(8,128)} %param.7) | copy-start | bytes 1966084
  44.7 21.3 %copy-start = (f32[5,8,16,512]{3,2,1,0:T(8,128)S(1)}, f32[5,8,16,512]{3,2,1,0:T(8,128)}, u32[]{:S(2)}) copy-start(f32[5,8,16,512]{3,2,1,0:T(8,128)} %param.6) | copy-start | bytes 3932164
  44.7 324.6 %all-to-all-start = ((f32[32,1,40960]{2,1,0:T(1,128)}), f32[32,1,40960]{2,1,0:T(1,128)}, u32[]{:S(2)}, u32[]{:S(2)}) async-start(f32[32,1,40960]{2,1,0:T(1,128)} %reshape.135), calls=%async_computation | async-start | bytes 10485760 | tf_op jit(solution)/shard_map/all_to_all | solution.py:90
  55.9 13.0 %copy-start.10 = (s32[32]{0:T(128)S(1)}, s32[32]{0:T(128)}, u32[]{:S(2)}) copy-start(s32[32]{0:T(128)} %param.8) | copy-start | bytes 388
  56.0 166.8 %collective-permute-start.8 = (f32[5,4,16,1]{3,2,1,0:T(8,128)S(1)}, f32[5,4,16,1]{3,2,1,0:T(8,128)S(1)}, u32[]{:S(2)}, u32[]{:S(2)}) collective-permute-start(f32[5,4,16,1]{3,2,1,0:T(8,128)S(1)} %get-tuple-element.17), channel_id=1, source_target_pairs={{0,8},{8,16},{16,24},{24,32},{32,40},{40,48},{48,56},{56,64},{64,7... | collective-permute-start | bytes 3848 | tf_op jit(solution)/shard_map/ppermute | solution.py:18
  57.7 165.1 %collective-permute-start.9 = (f32[5,4,16,1]{3,2,1,0:T(8,128)S(1)}, f32[5,4,16,1]{3,2,1,0:T(8,128)S(1)}, u32[]{:S(2)}, u32[]{:S(2)}) collective-permute-start(f32[5,4,16,1]{3,2,1,0:T(8,128)S(1)} %get-tuple-element.18), channel_id=1, source_target_pairs={{8,0},{16,8},{24,16},{32,24},{40,32},{48,40},{56,48},{64,56},{72,6... | collective-permute-start | bytes 3848 | tf_op jit(solution)/shard_map/ppermute | solution.py:20
  58.4 192.1 %collective-permute-start.6 = (f32[5,4,1,512]{3,2,1,0:T(1,128)}, f32[5,4,1,512]{3,2,1,0:T(1,128)S(1)}, u32[]{:S(2)}, u32[]{:S(2)}) collective-permute-start(f32[5,4,1,512]{3,2,1,0:T(1,128)} %get-tuple-element.15), channel_id=1, source_target_pairs={{0,1},{1,2},{2,3},{3,4},{4,5},{5,6},{6,7},{8,9},{9,10},{10,11},{11... | collective-permute-start | bytes 122888 | tf_op jit(solution)/shard_map/ppermute | solution.py:18
  64.6 185.9 %collective-permute-start.7 = (f32[5,4,1,512]{3,2,1,0:T(1,128)}, f32[5,4,1,512]{3,2,1,0:T(1,128)S(1)}, u32[]{:S(2)}, u32[]{:S(2)}) collective-permute-start(f32[5,4,1,512]{3,2,1,0:T(1,128)} %get-tuple-element.16), channel_id=1, source_target_pairs={{1,0},{2,1},{3,2},{4,3},{5,4},{6,5},{7,6},{9,8},{10,9},{11,10},{12... | collective-permute-start | bytes 122888 | tf_op jit(solution)/shard_map/ppermute | solution.py:20
  66.9 165.2 %collective-permute-start.3 = (f32[5,8,16,1]{3,2,1,0:T(8,128)}, f32[5,8,16,1]{3,2,1,0:T(8,128)S(1)}, u32[]{:S(2)}, u32[]{:S(2)}) collective-permute-start(f32[5,8,16,1]{3,2,1,0:T(8,128)} %get-tuple-element.11), channel_id=1, source_target_pairs={{0,8},{8,16},{16,24},{24,32},{32,40},{40,48},{48,56},{56,64},{64,7... | collective-permute-start | bytes 7688 | tf_op jit(solution)/shard_map/ppermute | solution.py:18
  222.8 23.2 %collective-permute-start.4 = (f32[5,8,16,1]{3,2,1,0:T(8,128)}, f32[5,8,16,1]{3,2,1,0:T(8,128)S(1)}, u32[]{:S(2)}, u32[]{:S(2)}) collective-permute-start(f32[5,8,16,1]{3,2,1,0:T(8,128)} %get-tuple-element.12), channel_id=1, source_target_pairs={{8,0},{16,8},{24,16},{32,24},{40,32},{48,40},{56,48},{64,56},{72,6... | collective-permute-start | bytes 7688 | tf_op jit(solution)/shard_map/ppermute | solution.py:20
  222.8 29.2 %collective-permute-start.1 = (f32[5,8,1,512]{3,1,2,0:T(8,128)}, f32[5,8,1,512]{3,1,2,0:T(8,128)S(1)}, u32[]{:S(2)}, u32[]{:S(2)}) collective-permute-start(f32[5,8,1,512]{3,1,2,0:T(8,128)} %copy.29), channel_id=1, source_target_pairs={{0,1},{1,2},{2,3},{3,4},{4,5},{5,6},{6,7},{8,9},{9,10},{10,11},{11... | collective-permute-start | bytes 245768 | tf_op jit(solution)/shard_map/ppermute | solution.py:18
  230.8 1.3 copy-start.9
  232.1 19.9 %collective-permute-start.2 = (f32[5,8,1,512]{3,1,2,0:T(8,128)S(1)}, f32[5,8,1,512]{3,1,2,0:T(8,128)S(1)}, u32[]{:S(2)}, u32[]{:S(2)}) collective-permute-start(f32[5,8,1,512]{3,1,2,0:T(8,128)S(1)} %copy-done.9), channel_id=1, source_target_pairs={{1,0},{2,1},{3,2},{4,3},{5,4},{6,5},{7,6},{9,8},{10,9},{11,10},{12... | collective-permute-start | bytes 245768 | tf_op jit(solution)/shard_map/ppermute | solution.py:20
  464.7 13.5 %copy-start.7 = (f32[8,16,512]{2,1,0:T(8,128)S(1)}, f32[8,16,512]{2,1,0:T(8,128)}, u32[]{:S(2)}) copy-start(f32[8,16,512]{2,1,0:T(8,128)} %multiply_bitcast_fusion) | copy-start | bytes 786436
  464.7 18.3 %collective-permute-start.5 = (f32[5,16,512]{2,1,0:T(8,128)}, f32[5,16,512]{2,1,0:T(8,128)}, u32[]{:S(2)}, u32[]{:S(2)}) collective-permute-start(f32[5,16,512]{2,1,0:T(8,128)} %reshape.112), channel_id=1, source_target_pairs={{0,8},{8,16},{16,24},{24,32},{32,40},{40,48},{48,56},{56,64},{64,7... | collective-permute-start | bytes 491528 | tf_op jit(solution)/shard_map/ppermute | solution.py:30
  478.2 1.4 copy-start.3
  478.2 2.0 copy-start.4
  478.5 2.3 copy-start.2
  480.8 3.3 copy-start.8
  484.1 1.1 copy-start.5
  484.1 1.4 copy-start.6
Sparse Core Ops, SparseCore 0:
  14.8 351.4 all-gather.1
